TPU v7x, 256 devices: a whole 4x4x8 slice. The times are simulated.
256 devices in a mesh: bench: 32 (over x, y, core), sweep: 8 (over z).
Axes of the slice: x: 4, y: 4, z: 8, core: 2. Of those that a mesh axis runs over, the one named last changes fastest.
Arguments:
- finished: bfloat16 [1024, 8, 64, 128], P('bench', 'sweep'), may hold values from -6 to 6
- noise: bfloat16 [1024, 8, 64, 128], P('bench', 'sweep'), may hold values from -6 to 6
- factors: bfloat16 [1024, 8, 8, 128, 128], P('bench', 'sweep'), may hold values from -0.1875 to 0.1875
- chol: bfloat16 [1024, 8, 128, 128], P('bench', 'sweep'), may hold values from -0.1875 to 0.1875
- front_w: bfloat16 [1024, 8, 128, 128], P('bench', 'sweep'), may hold values from -0.5 to 0.5
- parents: int32 [1024, 8, 8], P('bench', 'sweep'), may hold values from 0 to 1023, as said below
Outputs:
- evolved: float32 [1024, 8, 64, 128], P('bench', 'sweep')
Inputs may be any that keep to these rules, and one draw needn't show every extreme that they name: A parent row p lies on the bench owner p // 32. The 256 parents of the tiles of one bench group and sweep column name at most 16 rows of one owner, exactly 16 for some owner, and lie on at most 17 owners.
All inputs are finite; a program needn't handle non-finite values.
Results may differ from a plain program's by a relative error of at most 0.0003.
Values may be sent and summed in bfloat16 or wider, within the bound.
No kernel may reach another device: no remote copies, remote signals or barrier semaphores. Data moves between devices by JAX's collectives and lax.ppermute only.
A program may use at most 128 MiB of HBM per device.

v0:
```python
import jax
import jax.numpy as jnp
from jax import lax
from jax.sharding import PartitionSpec as P


def from_behind(array, axis, by):
    size = lax.axis_size(axis)
    pairs = [(i, i + by) for i in range(size) if 0 <= i + by < size]
    return lax.ppermute(array, axis, pairs)


def body(finished, noise, factors, chol, front_w, parents):
    pool_local = finished[:, 0]
    tile_count = noise.shape[0]
    fan = parents.shape[2]
    wanted = parents[:, 0].reshape(-1)
    whole_pool = lax.all_gather(finished, "bench", axis=0, tiled=True)
    chosen = jnp.take(whole_pool[:, 0], wanted, axis=0)
    chosen = chosen.reshape((tile_count, fan) + pool_local.shape[1:])
    local = jnp.einsum("jkrm,jkmn->jrn", chosen, factors[:, 0], preferred_element_type=jnp.float32)
    local = local + jnp.einsum(
        "jrm,jmn->jrn", noise[:, 0], chol[:, 0], preferred_element_type=jnp.float32
    )
    weights = front_w[:, 0].astype(jnp.float32)
    last_weight = weights[tile_count - 1]
    last_local = local[tile_count - 1]
    incoming = jnp.zeros_like(last_local)
    outgoing = last_local
    for step in range(lax.axis_size("sweep") - 1):
        incoming = from_behind(outgoing, "sweep", 1)
        outgoing = last_local + jnp.dot(incoming, last_weight, precision=lax.Precision.HIGHEST)
    tiles = local + jnp.einsum("rm,jmn->jrn", incoming, weights, precision=lax.Precision.HIGHEST)
    return tiles[:, None]


def solution(mesh):
    return jax.shard_map(
        body,
        mesh=mesh,
        in_specs=(
            P("bench", "sweep", None, None),
            P("bench", "sweep", None, None),
            P("bench", "sweep", None, None, None),
            P("bench", "sweep", None, None),
            P("bench", "sweep", None, None),
            P("bench", "sweep", None),
        ),
        out_specs=P("bench", "sweep", None, None),
        check_vma=False,
    )
```

profile of v0, /device:TPU:128, one launch (start us, length us, event | category | flops | bytes accessed | tf_op | source)
XLA Modules:
  0.0 163.4 jit_solution(4601643470623711922)
XLA Ops:
  6.5 0.0 copy-start
  6.5 0.0 all-gather.2.cloned.1.call-start
  6.5 0.7 all-gather.2.cloned.1.call-update
  7.3 0.8 copy.13
  8.0 0.1 reshape_squeeze.6
  8.1 0.7 compare_and_fusion
  8.8 0.1 copy.12
  8.9 80.1 %all-gather.2.cloned.1.call-done = bf16[1024,1,64,128]{3,2,1,0:T(8,128)(2,1)} async-done(((bf16[32,1,64,128]{3,2,1,0:T(8,128)(2,1)}), bf16[1024,1,64,128]{3,2,1,0:T(8,128)(2,1)}) %all-gather.2.cloned.1.call-update) | async-done | bytes 16777232 | tf_op jit(solution)/shard_map/all_gather | solution.py:18
  89.0 8.8 %gather_fusion = bf16[256,64,128]{2,1,0:T(8,128)(2,1)} fusion(bf16[1024,64,128]{2,1,0:T(8,128)(2,1)} %bitcast.73, s32[1024]{0:T(1024)S(1)} %pad_clamp_fusion), kind=kCustom, calls=%fused_computation | custom fusion | bytes 8389632 | tf_op jit(solution)/shard_map/jit(_take)/gather | solution.py:19
  97.8 0.0 copy-start.2
  97.8 0.0 copy-start.1
  97.8 6.6 %fusion.7 = f32[32,64,128]{2,1,0:T(8,128)S(1)} fusion(bf16[32,1,8,128,128]{4,3,2,1,0:T(8,128)(2,1)} %param.8, bf16[32,8,64,128]{3,2,1,0:T(8,128)(2,1)} %bitcast.72, pred[32,8]{1,0:T(8,128)(4,1)S(1)} %copy.12), kind=kOutput, calls=%fused_computation.10 | convolution fusion | flops 538968064 | bytes 13631744 | tf_op jit(solution)/shard_map/jkrm,jkmn->jrn/dot_general | solution.py:21
  104.4 0.0 copy-done
  104.4 0.0 copy-done.2
  104.4 0.4 convolution_add_fusion
  104.9 2.6 %collective-permute-start = (f32[64,128]{1,0:T(8,128)S(1)}, f32[64,128]{1,0:T(8,128)S(1)}, u32[]{:S(2)}, u32[]{:S(2)}) collective-permute-start(f32[64,128]{1,0:T(8,128)S(1)} %slice_bitcast_fusion), channel_id=1, source_target_pairs={{0,1},{1,2},{2,3},{3,4},{4,5},{5,6},{6,7},{8,9},{9,10},{10,11},{11... | collective-permute-start | bytes 98312 | tf_op jit(solution)/shard_map/ppermute | solution.py:10
  107.5 4.4 %collective-permute-done = f32[64,128]{1,0:T(8,128)S(1)} collective-permute-done((f32[64,128]{1,0:T(8,128)S(1)}, f32[64,128]{1,0:T(8,128)S(1)}, u32[]{:S(2)}, u32[]{:S(2)}) %collective-permute-start) | collective-permute-done | bytes 32800 | tf_op jit(solution)/shard_map/ppermute | solution.py:10
  111.9 0.0 copy-done.1
  111.9 0.2 convolution_add_fusion.6
  112.1 1.9 %collective-permute-start.1 = (f32[64,128]{1,0:T(8,128)S(1)}, f32[64,128]{1,0:T(8,128)S(1)}, u32[]{:S(2)}, u32[]{:S(2)}) collective-permute-start(f32[64,128]{1,0:T(8,128)S(1)} %convolution_add_fusion.6), channel_id=1, source_target_pairs={{0,1},{1,2},{2,3},{3,4},{4,5},{5,6},{6,7},{8,9},{9,10},{10,11},{11... | collective-permute-start | bytes 98312 | tf_op jit(solution)/shard_map/ppermute | solution.py:10
  114.0 5.1 %collective-permute-done.1 = f32[64,128]{1,0:T(8,128)S(1)} collective-permute-done((f32[64,128]{1,0:T(8,128)S(1)}, f32[64,128]{1,0:T(8,128)S(1)}, u32[]{:S(2)}, u32[]{:S(2)}) %collective-permute-start.1) | collective-permute-done | bytes 32800 | tf_op jit(solution)/shard_map/ppermute | solution.py:10
  119.1 0.2 convolution_add_fusion.5
  119.3 1.9 %collective-permute-start.2 = (f32[64,128]{1,0:T(8,128)S(1)}, f32[64,128]{1,0:T(8,128)S(1)}, u32[]{:S(2)}, u32[]{:S(2)}) collective-permute-start(f32[64,128]{1,0:T(8,128)S(1)} %convolution_add_fusion.5), channel_id=1, source_target_pairs={{0,1},{1,2},{2,3},{3,4},{4,5},{5,6},{6,7},{8,9},{9,10},{10,11},{11... | collective-permute-start | bytes 98312 | tf_op jit(solution)/shard_map/ppermute | solution.py:10
  121.2 5.1 %collective-permute-done.2 = f32[64,128]{1,0:T(8,128)S(1)} collective-permute-done((f32[64,128]{1,0:T(8,128)S(1)}, f32[64,128]{1,0:T(8,128)S(1)}, u32[]{:S(2)}, u32[]{:S(2)}) %collective-permute-start.2) | collective-permute-done | bytes 32800 | tf_op jit(solution)/shard_map/ppermute | solution.py:10
  126.3 0.2 convolution_add_fusion.4
  126.5 1.9 %collective-permute-start.3 = (f32[64,128]{1,0:T(8,128)S(1)}, f32[64,128]{1,0:T(8,128)S(1)}, u32[]{:S(2)}, u32[]{:S(2)}) collective-permute-start(f32[64,128]{1,0:T(8,128)S(1)} %convolution_add_fusion.4), channel_id=1, source_target_pairs={{0,1},{1,2},{2,3},{3,4},{4,5},{5,6},{6,7},{8,9},{9,10},{10,11},{11... | collective-permute-start | bytes 98312 | tf_op jit(solution)/shard_map/ppermute | solution.py:10
  128.4 5.1 %collective-permute-done.3 = f32[64,128]{1,0:T(8,128)S(1)} collective-permute-done((f32[64,128]{1,0:T(8,128)S(1)}, f32[64,128]{1,0:T(8,128)S(1)}, u32[]{:S(2)}, u32[]{:S(2)}) %collective-permute-start.3) | collective-permute-done | bytes 32800 | tf_op jit(solution)/shard_map/ppermute | solution.py:10
  133.5 0.2 convolution_add_fusion.3
  133.6 1.9 %collective-permute-start.4 = (f32[64,128]{1,0:T(8,128)S(1)}, f32[64,128]{1,0:T(8,128)S(1)}, u32[]{:S(2)}, u32[]{:S(2)}) collective-permute-start(f32[64,128]{1,0:T(8,128)S(1)} %convolution_add_fusion.3), channel_id=1, source_target_pairs={{0,1},{1,2},{2,3},{3,4},{4,5},{5,6},{6,7},{8,9},{9,10},{10,11},{11... | collective-permute-start | bytes 98312 | tf_op jit(solution)/shard_map/ppermute | solution.py:10
  135.6 5.1 %collective-permute-done.4 = f32[64,128]{1,0:T(8,128)S(1)} collective-permute-done((f32[64,128]{1,0:T(8,128)S(1)}, f32[64,128]{1,0:T(8,128)S(1)}, u32[]{:S(2)}, u32[]{:S(2)}) %collective-permute-start.4) | collective-permute-done | bytes 32800 | tf_op jit(solution)/shard_map/ppermute | solution.py:10
  140.7 0.2 convolution_add_fusion.2
  140.8 1.9 %collective-permute-start.5 = (f32[64,128]{1,0:T(8,128)S(1)}, f32[64,128]{1,0:T(8,128)S(1)}, u32[]{:S(2)}, u32[]{:S(2)}) collective-permute-start(f32[64,128]{1,0:T(8,128)S(1)} %convolution_add_fusion.2), channel_id=1, source_target_pairs={{0,1},{1,2},{2,3},{3,4},{4,5},{5,6},{6,7},{8,9},{9,10},{10,11},{11... | collective-permute-start | bytes 98312 | tf_op jit(solution)/shard_map/ppermute | solution.py:10
  142.8 5.1 %collective-permute-done.5 = f32[64,128]{1,0:T(8,128)S(1)} collective-permute-done((f32[64,128]{1,0:T(8,128)S(1)}, f32[64,128]{1,0:T(8,128)S(1)}, u32[]{:S(2)}, u32[]{:S(2)}) %collective-permute-start.5) | collective-permute-done | bytes 32800 | tf_op jit(solution)/shard_map/ppermute | solution.py:10
  147.9 0.2 convolution_add_fusion.1
  148.0 1.9 %collective-permute-start.6 = (f32[64,128]{1,0:T(8,128)S(1)}, f32[64,128]{1,0:T(8,128)S(1)}, u32[]{:S(2)}, u32[]{:S(2)}) collective-permute-start(f32[64,128]{1,0:T(8,128)S(1)} %convolution_add_fusion.1), channel_id=1, source_target_pairs={{0,1},{1,2},{2,3},{3,4},{4,5},{5,6},{6,7},{8,9},{9,10},{10,11},{11... | collective-permute-start | bytes 98312 | tf_op jit(solution)/shard_map/ppermute | solution.py:10
  150.0 5.1 %collective-permute-done.6 = f32[64,128]{1,0:T(8,128)S(1)} collective-permute-done((f32[64,128]{1,0:T(8,128)S(1)}, f32[64,128]{1,0:T(8,128)S(1)}, u32[]{:S(2)}, u32[]{:S(2)}) %collective-permute-start.6) | collective-permute-done | bytes 32800 | tf_op jit(solution)/shard_map/ppermute | solution.py:10
  155.0 1.5 fusion.6
  (3 shorter events, 0.0 us)
Async XLA Ops:
  6.5 97.9 %copy-start = (bf16[32,1,128,128]{3,2,1,0:T(8,128)(2,1)S(1)}, bf16[32,1,128,128]{3,2,1,0:T(8,128)(2,1)}, u32[]{:S(2)}) copy-start(bf16[32,1,128,128]{3,2,1,0:T(8,128)(2,1)} %param.9) | copy-start | bytes 3145732
  6.5 82.4 %all-gather.2.cloned.1.call-start = ((), (), s32[]{:S(2)}) async-start(), calls=%async_computation | async-start | bytes 17301504 | tf_op jit(solution)/shard_map/all_gather | solution.py:18
  97.8 6.6 %copy-start.2 = (bf16[32,1,64,128]{3,2,1,0:T(8,128)(2,1)S(1)}, bf16[32,1,64,128]{3,2,1,0:T(8,128)(2,1)}, u32[]{:S(2)}) copy-start(bf16[32,1,64,128]{3,2,1,0:T(8,128)(2,1)} %param.7) | copy-start | bytes 1572868
  97.8 14.1 %copy-start.1 = (bf16[32,1,128,128]{3,2,1,0:T(8,128)(2,1)S(1)}, bf16[32,1,128,128]{3,2,1,0:T(8,128)(2,1)}, u32[]{:S(2)}) copy-start(bf16[32,1,128,128]{3,2,1,0:T(8,128)(2,1)} %param.10) | copy-start | bytes 3145732
  104.9 7.0 %collective-permute-start = (f32[64,128]{1,0:T(8,128)S(1)}, f32[64,128]{1,0:T(8,128)S(1)}, u32[]{:S(2)}, u32[]{:S(2)}) collective-permute-start(f32[64,128]{1,0:T(8,128)S(1)} %slice_bitcast_fusion), channel_id=1, source_target_pairs={{0,1},{1,2},{2,3},{3,4},{4,5},{5,6},{6,7},{8,9},{9,10},{10,11},{11... | collective-permute-start | bytes 98312 | tf_op jit(solution)/shard_map/ppermute | solution.py:10
  112.1 7.0 %collective-permute-start.1 = (f32[64,128]{1,0:T(8,128)S(1)}, f32[64,128]{1,0:T(8,128)S(1)}, u32[]{:S(2)}, u32[]{:S(2)}) collective-permute-start(f32[64,128]{1,0:T(8,128)S(1)} %convolution_add_fusion.6), channel_id=1, source_target_pairs={{0,1},{1,2},{2,3},{3,4},{4,5},{5,6},{6,7},{8,9},{9,10},{10,11},{11... | collective-permute-start | bytes 98312 | tf_op jit(solution)/shard_map/ppermute | solution.py:10
  119.3 7.0 %collective-permute-start.2 = (f32[64,128]{1,0:T(8,128)S(1)}, f32[64,128]{1,0:T(8,128)S(1)}, u32[]{:S(2)}, u32[]{:S(2)}) collective-permute-start(f32[64,128]{1,0:T(8,128)S(1)} %convolution_add_fusion.5), channel_id=1, source_target_pairs={{0,1},{1,2},{2,3},{3,4},{4,5},{5,6},{6,7},{8,9},{9,10},{10,11},{11... | collective-permute-start | bytes 98312 | tf_op jit(solution)/shard_map/ppermute | solution.py:10
  126.5 7.0 %collective-permute-start.3 = (f32[64,128]{1,0:T(8,128)S(1)}, f32[64,128]{1,0:T(8,128)S(1)}, u32[]{:S(2)}, u32[]{:S(2)}) collective-permute-start(f32[64,128]{1,0:T(8,128)S(1)} %convolution_add_fusion.4), channel_id=1, source_target_pairs={{0,1},{1,2},{2,3},{3,4},{4,5},{5,6},{6,7},{8,9},{9,10},{10,11},{11... | collective-permute-start | bytes 98312 | tf_op jit(solution)/shard_map/ppermute | solution.py:10
  133.6 7.0 %collective-permute-start.4 = (f32[64,128]{1,0:T(8,128)S(1)}, f32[64,128]{1,0:T(8,128)S(1)}, u32[]{:S(2)}, u32[]{:S(2)}) collective-permute-start(f32[64,128]{1,0:T(8,128)S(1)} %convolution_add_fusion.3), channel_id=1, source_target_pairs={{0,1},{1,2},{2,3},{3,4},{4,5},{5,6},{6,7},{8,9},{9,10},{10,11},{11... | collective-permute-start | bytes 98312 | tf_op jit(solution)/shard_map/ppermute | solution.py:10
  140.8 7.0 %collective-permute-start.5 = (f32[64,128]{1,0:T(8,128)S(1)}, f32[64,128]{1,0:T(8,128)S(1)}, u32[]{:S(2)}, u32[]{:S(2)}) collective-permute-start(f32[64,128]{1,0:T(8,128)S(1)} %convolution_add_fusion.2), channel_id=1, source_target_pairs={{0,1},{1,2},{2,3},{3,4},{4,5},{5,6},{6,7},{8,9},{9,10},{10,11},{11... | collective-permute-start | bytes 98312 | tf_op jit(solution)/shard_map/ppermute | solution.py:10
  148.0 7.0 %collective-permute-start.6 = (f32[64,128]{1,0:T(8,128)S(1)}, f32[64,128]{1,0:T(8,128)S(1)}, u32[]{:S(2)}, u32[]{:S(2)}) collective-permute-start(f32[64,128]{1,0:T(8,128)S(1)} %convolution_add_fusion.1), channel_id=1, source_target_pairs={{0,1},{1,2},{2,3},{3,4},{4,5},{5,6},{6,7},{8,9},{9,10},{10,11},{11... | collective-permute-start | bytes 98312 | tf_op jit(solution)/shard_map/ppermute | solution.py:10
Sparse Core Ops, SparseCore 0:
  9.9 79.0 all-gather.1
where the time goes:
time: 164 us; the launch traced here: 163 us
  waiting for transfers between devices  116 us (71%)
  starting transfers between devices  14.1 us (9%)
  between operations  13.5 us (8%)
  local copies, waits for them, and re-layouts  9.77 us (6%)
  matrix products  9.56 us (6%)
    all_gather x1, waiting for transfers between devices, body(): whole_pool = lax.all_gather(finished, 'bench', axis=0, tiled=True)  80.1 us
    ppermute x7, waiting for transfers between devices, from_behind(): return lax.ppermute(array, axis, pairs)  35 us
    ppermute x7, starting transfers between devices, from_behind(): return lax.ppermute(array, axis, pairs)  14.1 us
    gather x1, local copies, waits for them, and re-layouts, body(): chosen = jnp.take(whole_pool[:, 0], wanted, axis=0)  8.8 us
    dot_general x1, matrix products, body(): jnp.einsum('jkrm,jkmn->jrn', chosen, factors[:, 0], preferred_element_typ...  6.61 us
  transfers between devices with their start and end apart: 8, of which 8 were waited for; matrix products, arithmetic and copies ran while one was open for 1% of the time, Pallas kernels for 0%

commit v1 on v0

v1 whole, which is shorter than its diff:
```python
import functools

import jax
import jax.numpy as jnp
import numpy as np
from jax import lax
from jax.experimental import pallas as pl
from jax.experimental.pallas import tpu as pltpu
from jax.sharding import PartitionSpec as P


SIDE = 4
ORDER = (
    (0, 0, None), (-1, 0, None), (1, 0, None), (0, -1, None), (0, 1, None), (-1, -1, None),
    (-1, 1, None), (1, -1, None), (1, 1, None), (2, 0, None), (0, 2, None), (2, -1, None),
    (2, 1, None), (-1, 2, None), (1, 2, None), (2, 2, 0), (2, 2, 1),
)
BLOCKS = len(ORDER)
EARLY = (13, 11)


def place(x, y, core):
    return ((x % SIDE) * SIDE + y % SIDE) * 2 + core


def offset(core, a, b):
    return (a, b) if core == 0 else (-b, -a)


def fetch(array, a, b):
    pairs = []
    for x in range(SIDE):
        for y in range(SIDE):
            for core in range(2):
                dx, dy = offset(core, a, b)
                pairs.append((place(x + dx, y + dy, core), place(x, y, core)))
    return lax.ppermute(array, "bench", pairs)


def from_partner(array):
    chips = SIDE * SIDE
    pairs = [(2 * i + core, 2 * i + 1 - core) for i in range(chips) for core in range(2)]
    return lax.ppermute(array, "bench", pairs)


def from_behind(array, by):
    size = lax.axis_size("sweep")
    return lax.ppermute(array, "sweep", [(i, (i + by) % size) for i in range(size)])


VIA = {
    (-1, 0, None): ((0, 0, None), (-1, 0)),
    (1, 0, None): ((0, 0, None), (1, 0)),
    (0, -1, None): ((0, 0, None), (0, -1)),
    (0, 1, None): ((0, 0, None), (0, 1)),
    (-1, -1, None): ((-1, 0, None), (0, -1)),
    (-1, 1, None): ((-1, 0, None), (0, 1)),
    (1, -1, None): ((1, 0, None), (0, -1)),
    (1, 1, None): ((1, 0, None), (0, 1)),
    (2, 0, None): ((-1, 0, None), (-1, 0)),
    (0, 2, None): ((0, -1, None), (0, -1)),
    (2, -1, None): ((2, 0, None), (0, -1)),
    (2, 1, None): ((2, 0, None), (0, 1)),
    (-1, 2, None): ((-1, -1, None), (0, -1)),
    (1, 2, None): ((1, 1, None), (0, 1)),
    (2, 2, 0): ((2, -1, None), (0, -1)),
    (2, 2, 1): ((2, 1, None), (0, 1)),
}


def spread(own, small):
    b = {(0, 0, None): own}
    for d, (source, step) in VIA.items():
        if d == (-1, -1, None):
            first = ORDER[1]
            b[first], small = lax.optimization_barrier((b[first], small))
        block = b[source]
        if d[2] is not None:
            block = jnp.split(block, 2)[d[2]]
        b[d] = fetch(block, *step)
    mine = [b[d] for d in ORDER]
    theirs = [from_partner(b[d]) for d in ORDER]
    return mine, theirs, small


def orders(parents, rows):
    number = np.zeros((2, SIDE, SIDE, 2), np.int32)
    for core in range(2):
        for i, (a, b, half) in enumerate(ORDER):
            dx, dy = offset(core, a, b)
            number[core, dx % SIDE, dy % SIDE, slice(None) if half is None else half] = i
    early, late = np.arange(EARLY[0]), np.arange(EARLY[0], BLOCKS)
    theirs_early, theirs_late = np.arange(EARLY[1]), np.arange(EARLY[1], BLOCKS)
    rank = np.zeros((2, BLOCKS), np.int32)
    for i, (other, block) in enumerate(
        [(0, j) for j in early] + [(1, j) for j in theirs_early]
        + [(0, j) for j in late] + [(1, j) for j in theirs_late]
    ):
        rank[other, block] = i
    table = np.zeros((2, 2, 2 * SIDE * SIDE), np.int32)
    for mine in range(2):
        for core in range(2):
            table[mine, core] = rank[int(mine != core)][number[core].reshape(-1)]
    me = lax.axis_index("bench")
    slots = parents.reshape(-1)
    count = slots.shape[0]
    owner = slots // rows
    dx = (owner // (2 * SIDE) - me // (2 * SIDE)) % SIDE
    dy = (owner // 2 - me // 2) % SIDE
    half = (slots % rows) // (rows // 2)
    spot = ((((me % 2) * 2 + owner % 2) * SIDE + dx) * SIDE + dy) * 2 + half
    flat = table.reshape(-1)
    key = jnp.sum(
        jnp.where(spot[None, :] == jnp.arange(flat.size)[:, None], jnp.asarray(flat)[:, None], 0), 0
    )
    slot = jnp.arange(count, dtype=jnp.int32)
    full = key * count + slot
    place_of = jnp.sum((full[:, None] < full[None, :]).astype(jnp.int32), 0)
    packed = slot * rows + slots % rows
    ranked = jnp.sum(jnp.where(place_of[:, None] == slot[None, :], packed[:, None], 0), 0)
    edges = jnp.arange(2 * BLOCKS + 8, dtype=jnp.int32)
    begins = jnp.sum((key[:, None] < edges[None, :]).astype(jnp.int32), 0)
    return begins.astype(jnp.int32), ranked.astype(jnp.int32)


UNROLL = 4


def move_rows(begins, ranked, blocks, first, shift, out):
    for p, block in enumerate(blocks):
        rows = block.shape[0]
        low, high = begins[first + p], begins[first + p + 1]

        def move(i, carry, block=block, low=low, high=high, rows=rows):
            at = [jnp.minimum(low + i * UNROLL + u, high - 1) for u in range(UNROLL)]
            entries = [ranked[j] for j in at]
            values = [block[e & (rows - 1)] for e in entries]
            for e, value in zip(entries, values, strict=True):
                out[e >> shift] = value
            return carry

        lax.fori_loop(0, (high - low + UNROLL - 1) >> 2, move, 0)


def one_tile(t, fan, rows, factors, noise, chol):
    node = factors.shape[-1]
    chosen = jnp.concatenate([rows[t * fan + k] for k in range(fan)], axis=1)
    total = jnp.dot(
        chosen, factors[t].reshape(fan * node, node), preferred_element_type=jnp.float32
    )
    return total + jnp.dot(noise[t], chol[t], preferred_element_type=jnp.float32)


def early_kernel(shift, begins, ranked, *refs):
    blocks, loads, rows, loaded, sem = refs[:-10], refs[-10:-6], refs[-6], refs[-5:-1], refs[-1]
    copies = [
        pltpu.make_async_copy(source, target, sem.at[i])
        for i, (source, target) in enumerate(zip(loads, loaded, strict=True))
    ]
    for copy in copies:
        copy.start()
    move_rows(begins, ranked, blocks, 0, shift, rows)
    for copy in copies:
        copy.wait()


def late_kernel(first, shift, begins, ranked, *refs):
    factors, noise, chol, _, rows, front = refs[-6:]
    count, fan = factors.shape[:2]
    move_rows(begins, ranked, refs[:-6], first, shift, rows)
    front[...] = one_tile(count - 1, fan, rows, factors, noise, chol)


def tiles_kernel(first, count, rows, factors, noise, chol, out):
    fan = factors.shape[1]

    def step(t, carry):
        out[t] = one_tile(first + t, fan, rows, factors, noise, chol)
        return carry

    lax.fori_loop(0, count, step, 0)


SMEM = pl.BlockSpec(memory_space=pltpu.SMEM)
VMEM = pl.BlockSpec(memory_space=pltpu.VMEM)
HBM = pl.BlockSpec(memory_space=pltpu.MemorySpace.HBM)
PARAMS = pltpu.CompilerParams(vmem_limit_bytes=8 * 1024 * 1024)


def cost(tiles_count, moved):
    return pl.CostEstimate(
        flops=2 * tiles_count * 64 * 128 * 128 * 9,
        bytes_accessed=moved,
        transcendentals=0,
    )


def shift_of(blocks):
    return max(block.shape[0] for block in blocks).bit_length() - 1


def gather_early(begins, ranked, blocks, slots, loads):
    shape = (slots,) + blocks[0].shape[1:]
    return pl.pallas_call(
        functools.partial(early_kernel, shift_of(blocks)),
        out_shape=[jax.ShapeDtypeStruct(shape, blocks[0].dtype)]
        + [jax.ShapeDtypeStruct(a.shape, a.dtype) for a in loads],
        in_specs=[SMEM, SMEM] + [VMEM] * len(blocks) + [HBM] * len(loads),
        out_specs=[VMEM] * (1 + len(loads)),
        scratch_shapes=[pltpu.SemaphoreType.DMA((len(loads),))],
        compiler_params=PARAMS,
        cost_estimate=cost(0, 16 << 20),
        name="early",
    )(begins, ranked, *blocks, *[pltpu.with_memory_space_constraint(a, pltpu.HBM) for a in loads])


def gather_late(begins, ranked, blocks, first, factors, noise, chol, rows):
    real, node = noise.shape[1:]
    return pl.pallas_call(
        functools.partial(late_kernel, first, shift_of(blocks)),
        out_shape=(
            jax.ShapeDtypeStruct(rows.shape, rows.dtype),
            jax.ShapeDtypeStruct((real, node), jnp.float32),
        ),
        in_specs=[SMEM, SMEM] + [VMEM] * (len(blocks) + 4),
        out_specs=(VMEM, VMEM),
        input_output_aliases={2 + len(blocks) + 3: 0},
        compiler_params=PARAMS,
        cost_estimate=cost(1, 4 << 20),
        name="late",
    )(begins, ranked, *blocks, factors, noise, chol, rows)


def tiles(first, count, rows, factors, noise, chol):
    real, node = noise.shape[1:]
    return pl.pallas_call(
        functools.partial(tiles_kernel, first, count),
        out_shape=jax.ShapeDtypeStruct((count, real, node), jnp.float32),
        in_specs=[VMEM] * 4,
        out_specs=VMEM,
        compiler_params=PARAMS,
        cost_estimate=cost(count, 1 << 20),
        name="tiles",
    )(rows, factors, noise, chol)


def exact(a, b):
    return jnp.dot(a, b, precision=lax.Precision.HIGHEST)


def whole(finished, noise, factors, chol, front_w, parents):
    own = finished[:, 0]
    noise, factors, chol = noise[:, 0], factors[:, 0], chol[:, 0]
    count, fan = factors.shape[0], factors.shape[1]
    position = lax.axis_index("sweep")
    small = orders(parents[:, 0], own.shape[0])
    small += tuple((position >= least).astype(jnp.float32) for least in (1, 2, 3, 4, 7))
    mine, theirs, small = spread(own, small)
    begins, ranked, *keep = small

    last_w = front_w[count - 1, 0]
    back1 = from_behind(last_w, 1).astype(jnp.float32)
    back2 = from_behind(last_w, 2).astype(jnp.float32)
    back3 = from_behind(last_w, 3).astype(jnp.float32)
    two = exact(back2, back1)
    three = exact(back3, two)
    six = exact(from_behind(three, 3), three)
    one, two, three, six = keep[1] * back1, keep[2] * two, keep[3] * three, keep[4] * six

    early = mine[: EARLY[0]] + theirs[: EARLY[1]]
    late = mine[EARLY[0] :] + theirs[EARLY[1] :]
    rows, factors, noise, chol, weights = gather_early(
        begins, ranked, early, count * fan, (factors, noise, chol, front_w[:, 0])
    )
    rows, front = gather_late(begins, ranked, late, len(early), factors, noise, chol, rows)
    cut = count // 2
    first = tiles(0, cut, rows, factors, noise, chol)
    second = tiles(cut, count - 1 - cut, rows, factors, noise, chol)
    near = [from_behind(front, by) for by in (1, 2, 3)]
    part = keep[0] * near[0] + exact(near[1], one) + exact(near[2], two)
    incoming = part + exact(from_behind(part, 3), three) + exact(from_behind(part, 6), six)
    local = jnp.concatenate([first, second, front[None]])
    weights = weights.astype(jnp.float32)
    out = local + jnp.einsum("rm,jmn->jrn", incoming, weights, precision=lax.Precision.HIGHEST)
    return out[:, None]


def solution(mesh):
    return jax.shard_map(
        whole,
        mesh=mesh,
        in_specs=(
            P("bench", "sweep", None, None),
            P("bench", "sweep", None, None),
            P("bench", "sweep", None, None, None),
            P("bench", "sweep", None, None),
            P("bench", "sweep", None, None),
            P("bench", "sweep", None),
        ),
        out_specs=P("bench", "sweep", None, None),
        check_vma=False,
    )
```

time: 164 us -> 115 us (0.70)
  the two profiles are of different devices: /device:TPU:128 before, /device:TPU:32 now
where the time goes in v1:
time: 115 us
  waiting for transfers between devices  48 us (42%)
  starting transfers between devices  47.8 us (42%)
  Pallas kernels  12 us (10%)
  matrix products  3.08 us (3%)
  local copies, waits for them, and re-layouts  2.69 us (2%)
  other arithmetic  1.19 us (1%)
    ppermute x16, waiting for transfers between devices, fetch(): return lax.ppermute(array, 'bench', pairs)  32.9 us
    ppermute x9, starting transfers between devices, from_behind(): lax.ppermute(array, 'sweep', [(i, (i + by) % size) for i in range(size)])  22.5 us
    ppermute x16, starting transfers between devices, fetch(): return lax.ppermute(array, 'bench', pairs)  21.5 us
    ppermute x9, waiting for transfers between devices, from_behind(): lax.ppermute(array, 'sweep', [(i, (i + by) % size) for i in range(size)])  11.9 us
    pallas_call x2, Pallas kernels, tiles(): pl.pallas_call(functools.partial(tiles_kernel, first, count), out_shape=j...  6 us
    pallas_call x1, Pallas kernels, gather_early(): pl.pallas_call(functools.partial(early_kernel, shift_of(blocks)), out_sha...  4.64 us
    ppermute x17, starting transfers between devices, from_partner(): return lax.ppermute(array, 'bench', pairs)  3.81 us
    ppermute x17, waiting for transfers between devices, from_partner(): return lax.ppermute(array, 'bench', pairs)  3.29 us
  transfers between devices with their start and end apart: 42, of which 13 were waited for; matrix products, arithmetic and copies ran while one was open for 4% of the time, Pallas kernels for 10%

profile of v1, /device:TPU:32, one launch (start us, length us, event | category | flops | bytes accessed | tf_op | source)
XLA Modules:
  0.0 115.1 jit_solution(13775047283427149053)
XLA Ops:
  0.0 1.5 %collective-permute-start = (bf16[32,64,128]{2,1,0:T(8,128)(2,1)}, bf16[32,64,128]{2,1,0:T(8,128)(2,1)S(1)}, u32[]{:S(2)}, u32[]{:S(2)}) collective-permute-start(bf16[32,64,128]{2,1,0:T(8,128)(2,1)} %bitcast.37), channel_id=1, source_target_pairs={{192,0},{24,8},{208,16},{40,24},{224,32},{56,40},{240,48},{8,56},{... | collective-permute-start | bytes 1572872 | tf_op jit(solution)/shard_map/ppermute | solution.py:37
  1.5 1.7 %collective-permute-start.3 = (bf16[32,64,128]{2,1,0:T(8,128)(2,1)}, bf16[32,64,128]{2,1,0:T(8,128)(2,1)S(1)}, u32[]{:S(2)}, u32[]{:S(2)}) collective-permute-start(bf16[32,64,128]{2,1,0:T(8,128)(2,1)} %bitcast.38), channel_id=1, source_target_pairs={{64,0},{56,8},{80,16},{8,24},{96,32},{24,40},{112,48},{40,56},{128... | collective-permute-start | bytes 1572872 | tf_op jit(solution)/shard_map/ppermute | solution.py:37
  3.2 1.6 %collective-permute-start.17 = (bf16[32,64,128]{2,1,0:T(8,128)(2,1)}, bf16[32,64,128]{2,1,0:T(8,128)(2,1)S(1)}, u32[]{:S(2)}, u32[]{:S(2)}) collective-permute-start(bf16[32,64,128]{2,1,0:T(8,128)(2,1)} %bitcast.39), channel_id=1, source_target_pairs={{48,0},{72,8},{0,16},{88,24},{16,32},{104,40},{32,48},{120,56},{11... | collective-permute-start | bytes 1572872 | tf_op jit(solution)/shard_map/ppermute | solution.py:37
  4.8 0.8 slice_bitcast_fusion
  5.6 1.9 %collective-permute-start.35 = (bf16[128,128]{1,0:T(8,128)(2,1)S(1)}, bf16[128,128]{1,0:T(8,128)(2,1)S(1)}, u32[]{:S(2)}, u32[]{:S(2)}) collective-permute-start(bf16[128,128]{1,0:T(8,128)(2,1)S(1)} %slice_bitcast_fusion), channel_id=1, source_target_pairs={{0,1},{1,2},{2,3},{3,4},{4,5},{5,6},{6,7},{7,0},{8,9},{9,10},{10,1... | collective-permute-start | bytes 98312 | tf_op jit(solution)/shard_map/ppermute | solution.py:48
  7.5 4.5 %collective-permute-start.37 = (bf16[128,128]{1,0:T(8,128)(2,1)S(1)}, bf16[128,128]{1,0:T(8,128)(2,1)S(1)}, u32[]{:S(2)}, u32[]{:S(2)}) collective-permute-start(bf16[128,128]{1,0:T(8,128)(2,1)S(1)} %slice_bitcast_fusion), channel_id=1, source_target_pairs={{0,2},{1,3},{2,4},{3,5},{4,6},{5,7},{6,0},{7,1},{8,10},{9,11},{10,... | collective-permute-start | bytes 98312 | tf_op jit(solution)/shard_map/ppermute | solution.py:48
  12.0 0.8 copy.12
  12.7 0.1 reshape_squeeze.3
  12.9 0.8 select_reduce_fusion.1
  13.6 0.1 convert_reduce_fusion
  13.8 0.2 select_reduce_fusion.ranked
  13.9 1.7 %collective-permute-start.18 = (bf16[32,64,128]{2,1,0:T(8,128)(2,1)}, bf16[32,64,128]{2,1,0:T(8,128)(2,1)S(1)}, u32[]{:S(2)}, u32[]{:S(2)}) collective-permute-start(bf16[32,64,128]{2,1,0:T(8,128)(2,1)} %bitcast.40), channel_id=1, source_target_pairs={{16,0},{200,8},{32,16},{216,24},{48,32},{232,40},{0,48},{248,56},{... | collective-permute-start | bytes 1572872 | tf_op jit(solution)/shard_map/ppermute | solution.py:37
  15.7 2.8 %collective-permute-start.39 = (bf16[128,128]{1,0:T(8,128)(2,1)S(1)}, bf16[128,128]{1,0:T(8,128)(2,1)S(1)}, u32[]{:S(2)}, u32[]{:S(2)}) collective-permute-start(bf16[128,128]{1,0:T(8,128)(2,1)S(1)} %slice_bitcast_fusion), channel_id=1, source_target_pairs={{0,3},{1,4},{2,5},{3,6},{4,7},{5,0},{6,1},{7,2},{8,11},{9,12},{10,... | collective-permute-start | bytes 98312 | tf_op jit(solution)/shard_map/ppermute | solution.py:48
  18.5 0.1 convert_reduce_fusion.1.begins
  18.6 4.7 %collective-permute-done.39 = bf16[128,128]{1,0:T(8,128)(2,1)S(1)} collective-permute-done((bf16[128,128]{1,0:T(8,128)(2,1)S(1)}, bf16[128,128]{1,0:T(8,128)(2,1)S(1)}, u32[]{:S(2)}, u32[]{:S(2)}) %collective-permute-start.39) | collective-permute-done | bytes 32800 | tf_op jit(solution)/shard_map/ppermute | solution.py:48
  23.3 1.0 collective-permute-start.1
  24.3 2.3 %collective-permute-start.19 = (bf16[32,64,128]{2,1,0:T(8,128)(2,1)S(1)}, bf16[32,64,128]{2,1,0:T(8,128)(2,1)S(1)}, u32[]{:S(2)}, u32[]{:S(2)}) collective-permute-start(bf16[32,64,128]{2,1,0:T(8,128)(2,1)S(1)} %collective-permute-done.refs_1_), channel_id=1, source_target_pairs={{16,0},{200,8},{32,16},{216,24},{48,32},{232,40},{0,48},{248,56},{... | collective-permute-start | bytes 1572872 | tf_op jit(solution)/shard_map/ppermute | solution.py:37
  26.5 0.1 collective-permute-start.6
  26.7 0.9 collective-permute-start.4
  27.6 6.1 %collective-permute-done.1.refs_5_ = bf16[32,64,128]{2,1,0:T(8,128)(2,1)S(1)} collective-permute-done((bf16[32,64,128]{2,1,0:T(8,128)(2,1)S(1)}, bf16[32,64,128]{2,1,0:T(8,128)(2,1)S(1)}, u32[]{:S(2)}, u32[]{:S(2)}) %collective-permute-start.1) | collective-permute-done | bytes 524320 | tf_op jit(solution)/shard_map/ppermute | solution.py:37
  33.7 4.9 %collective-permute-done.19.refs_6_ = bf16[32,64,128]{2,1,0:T(8,128)(2,1)S(1)} collective-permute-done((bf16[32,64,128]{2,1,0:T(8,128)(2,1)S(1)}, bf16[32,64,128]{2,1,0:T(8,128)(2,1)S(1)}, u32[]{:S(2)}, u32[]{:S(2)}) %collective-permute-start.19) | collective-permute-done | bytes 524320 | tf_op jit(solution)/shard_map/ppermute | solution.py:37
  38.6 0.9 collective-permute-start.21
  39.4 3.1 %collective-permute-done.6.refs_9_ = bf16[32,64,128]{2,1,0:T(8,128)(2,1)S(1)} collective-permute-done((bf16[32,64,128]{2,1,0:T(8,128)(2,1)S(1)}, bf16[32,64,128]{2,1,0:T(8,128)(2,1)S(1)}, u32[]{:S(2)}, u32[]{:S(2)}) %collective-permute-start.6) | collective-permute-done | bytes 524320 | tf_op jit(solution)/shard_map/ppermute | solution.py:37
  42.6 0.5 collective-permute-start.25
  43.1 1.1 collective-permute-done.4.refs_8_
  44.2 0.9 collective-permute-start.26
  45.1 4.6 %collective-permute-done.21.refs_10_ = bf16[32,64,128]{2,1,0:T(8,128)(2,1)S(1)} collective-permute-done((bf16[32,64,128]{2,1,0:T(8,128)(2,1)S(1)}, bf16[32,64,128]{2,1,0:T(8,128)(2,1)S(1)}, u32[]{:S(2)}, u32[]{:S(2)}) %collective-permute-start.21) | collective-permute-done | bytes 524320 | tf_op jit(solution)/shard_map/ppermute | solution.py:37
  49.7 0.5 collective-permute-start.31
  50.2 3.2 %collective-permute-start.9 = (bf16[32,64,128]{2,1,0:T(8,128)(2,1)S(1)}, bf16[32,64,128]{2,1,0:T(8,128)(2,1)S(1)}, u32[]{:S(2)}, u32[]{:S(2)}) collective-permute-start(bf16[32,64,128]{2,1,0:T(8,128)(2,1)S(1)} %collective-permute-done.6.refs_9_), channel_id=1, source_target_pairs={{16,0},{200,8},{32,16},{216,24},{48,32},{232,40},{0,48},{248,56},{... | collective-permute-start | bytes 1572872 | tf_op jit(solution)/shard_map/ppermute | solution.py:37
  53.5 0.5 collective-permute-start.29
  54.0 0.1 collective-permute-start.32
  54.1 6.5 %collective-permute-done.7.refs_11_ = bf16[32,64,128]{2,1,0:T(8,128)(2,1)S(1)} collective-permute-done((bf16[32,64,128]{2,1,0:T(8,128)(2,1)S(1)}, bf16[32,64,128]{2,1,0:T(8,128)(2,1)S(1)}, u32[]{:S(2)}, u32[]{:S(2)}) %collective-permute-start.7) | collective-permute-done | bytes 524320 | tf_op jit(solution)/shard_map/ppermute | solution.py:37
  60.6 3.2 %collective-permute-start.5 = (bf16[32,64,128]{2,1,0:T(8,128)(2,1)S(1)}, bf16[32,64,128]{2,1,0:T(8,128)(2,1)S(1)}, u32[]{:S(2)}, u32[]{:S(2)}) collective-permute-start(bf16[32,64,128]{2,1,0:T(8,128)(2,1)S(1)} %collective-permute-done.4.refs_8_), channel_id=1, source_target_pairs={{16,0},{200,8},{32,16},{216,24},{48,32},{232,40},{0,48},{248,56},{... | collective-permute-start | bytes 1572872 | tf_op jit(solution)/shard_map/ppermute | solution.py:37
  63.9 0.1 collective-permute-start.8
  64.0 3.3 %collective-permute-start.10 = (bf16[16,64,128]{2,1,0:T(8,128)(2,1)S(1)}, bf16[16,64,128]{2,1,0:T(8,128)(2,1)S(1)}, u32[]{:S(2)}, u32[]{:S(2)}) collective-permute-start(bf16[16,64,128]{2,1,0:T(8,128)(2,1)S(1)} %split.9), channel_id=1, source_target_pairs={{16,0},{200,8},{32,16},{216,24},{48,32},{232,40},{0,48},{248,56},{... | collective-permute-start | bytes 786440 | tf_op jit(solution)/shard_map/ppermute | solution.py:37
  67.3 6.5 %collective-permute-done.8.refs_2_ = bf16[16,64,128]{2,1,0:T(8,128)(2,1)S(1)} collective-permute-done((bf16[16,64,128]{2,1,0:T(8,128)(2,1)S(1)}, bf16[16,64,128]{2,1,0:T(8,128)(2,1)S(1)}, u32[]{:S(2)}, u32[]{:S(2)}) %collective-permute-start.8) | collective-permute-done | bytes 262176 | tf_op jit(solution)/shard_map/ppermute | solution.py:37
  73.8 0.5 collective-permute-start.11
  74.3 0.1 collective-permute-start.12
  74.4 0.4 collective-permute-start.13
  74.8 0.1 collective-permute-start.14
  74.9 0.4 collective-permute-done.15.refs_8_
  75.3 0.1 collective-permute-start.16
  75.5 0.1 fusion.22
  75.6 0.3 fusion.23
  75.9 2.8 %collective-permute-done.16.refs_9_ = bf16[16,64,128]{2,1,0:T(8,128)(2,1)S(1)} collective-permute-done((bf16[16,64,128]{2,1,0:T(8,128)(2,1)S(1)}, bf16[16,64,128]{2,1,0:T(8,128)(2,1)S(1)}, u32[]{:S(2)}, u32[]{:S(2)}) %collective-permute-start.16) | collective-permute-done | bytes 262176 | tf_op jit(solution)/shard_map/ppermute | solution.py:43
  78.7 2.4 %collective-permute-start.41 = (f32[128,128]{0,1:T(8,128)S(1)}, f32[128,128]{0,1:T(8,128)S(1)}, u32[]{:S(2)}, u32[]{:S(2)}) collective-permute-start(f32[128,128]{0,1:T(8,128)S(1)} %bitcast.47), channel_id=1, source_target_pairs={{0,3},{1,4},{2,5},{3,6},{4,7},{5,0},{6,1},{7,2},{8,11},{9,12},{10,... | collective-permute-start | bytes 196616 | tf_op jit(solution)/shard_map/ppermute | solution.py:48
  81.1 1.0 copy-done
  82.1 4.6 %early.1 = (bf16[256,64,128]{2,1,0:T(8,128)(2,1)S(1)}, bf16[32,8,128,128]{3,2,1,0:T(8,128)(2,1)S(1)}, bf16[32,64,128]{2,1,0:T(8,128)(2,1)S(1)}, bf16[32,128,128]...) custom-call(s32[42]{0:T(128)S(1)} %convert_reduce_fusion.1.begins, s32[256]{0:T(256)S(1)} %select_reduce_fusion.ranked, ...), custom_call_target="tpu_custom_call" | custom-call | bytes 16777216 | tf_op jit(solution)/shard_map/early/pallas_call | solution.py:204
  86.8 1.3 %late.1 = (bf16[256,64,128]{2,1,0:T(8,128)(2,1)S(1)}, f32[64,128]{1,0:T(8,128)S(1)}) custom-call(s32[42]{0:T(128)S(1)} %convert_reduce_fusion.1.begins, s32[256]{0:T(256)S(1)} %select_reduce_fusion.ranked, bf16[32,64,128]{2,1,0:T(8,128)(2,1)S(1)} %collective-permute-done.2.refs_0_, ...), custom_call_target="tpu_custom_call", output_to_operand_aliasing={{0}: (15, {})} | custom-call | flops 18874368 | bytes 4194304 | tf_op jit(solution)/shard_map/late/pallas_call | solution.py:219
  88.3 0.3 fusion.24
  88.6 4.0 %collective-permute-start.34 = (f32[64,128]{1,0:T(8,128)S(1)}, f32[64,128]{1,0:T(8,128)S(1)}, u32[]{:S(2)}, u32[]{:S(2)}) collective-permute-start(f32[64,128]{1,0:T(8,128)S(1)} %get-tuple-element.28), channel_id=1, source_target_pairs={{0,2},{1,3},{2,4},{3,5},{4,6},{5,7},{6,0},{7,1},{8,10},{9,11},{10,... | collective-permute-start | bytes 98312 | tf_op jit(solution)/shard_map/ppermute | solution.py:48
  92.6 1.8 %collective-permute-start.33 = (f32[64,128]{1,0:T(8,128)S(1)}, f32[64,128]{1,0:T(8,128)S(1)}, u32[]{:S(2)}, u32[]{:S(2)}) collective-permute-start(f32[64,128]{1,0:T(8,128)S(1)} %get-tuple-element.28), channel_id=1, source_target_pairs={{0,1},{1,2},{2,3},{3,4},{4,5},{5,6},{6,7},{7,0},{8,9},{9,10},{10,1... | collective-permute-start | bytes 98312 | tf_op jit(solution)/shard_map/ppermute | solution.py:48
  94.4 1.0 collective-permute-done.36
  95.4 0.2 fusion.6
  95.6 1.2 %collective-permute-done.34 = f32[64,128]{1,0:T(8,128)S(1)} collective-permute-done((f32[64,128]{1,0:T(8,128)S(1)}, f32[64,128]{1,0:T(8,128)S(1)}, u32[]{:S(2)}, u32[]{:S(2)}) %collective-permute-start.34) | collective-permute-done | bytes 32800 | tf_op jit(solution)/shard_map/ppermute | solution.py:48
  96.8 0.2 fusion.8
  97.0 2.8 %collective-permute-start.40 = (f32[64,128]{1,0:T(8,128)S(1)}, f32[64,128]{1,0:T(8,128)S(1)}, u32[]{:S(2)}, u32[]{:S(2)}) collective-permute-start(f32[64,128]{1,0:T(8,128)S(1)} %add_add_fusion), channel_id=1, source_target_pairs={{0,6},{1,7},{2,0},{3,1},{4,2},{5,3},{6,4},{7,5},{8,14},{9,15},{10,... | collective-permute-start | bytes 98312 | tf_op jit(solution)/shard_map/ppermute | solution.py:48
  99.8 2.9 %tiles.3 = f32[15,64,128]{2,1,0:T(8,128)S(1)} custom-call(bf16[256,64,128]{2,1,0:T(8,128)(2,1)S(1)} %get-tuple-element.27.rows, bf16[32,8,128,128]{3,2,1,0:T(8,128)(2,1)S(1)} %get-tuple-element.23.refs_10_.factors, bf16[32,64,128]{2,1,0:T(8,128)(2,1)S(1)} %get-tuple-element.24.refs_11_.noise, bf16[32,128,128]{2,1,0:T(8,128)(2,1)S(1)} %get-tuple-element.25.refs_12_.chol), custom_call_target="tpu_custom_call" | custom-call | flops 283115520 | bytes 1048576 | tf_op jit(solution)/shard_map/tiles/pallas_call | solution.py:236
  102.7 3.1 %tiles.2 = f32[16,64,128]{2,1,0:T(8,128)S(1)} custom-call(bf16[256,64,128]{2,1,0:T(8,128)(2,1)S(1)} %get-tuple-element.27.rows, bf16[32,8,128,128]{3,2,1,0:T(8,128)(2,1)S(1)} %get-tuple-element.23.refs_10_.factors, bf16[32,64,128]{2,1,0:T(8,128)(2,1)S(1)} %get-tuple-element.24.refs_11_.noise, bf16[32,128,128]{2,1,0:T(8,128)(2,1)S(1)} %get-tuple-element.25.refs_12_.chol), custom_call_target="tpu_custom_call" | custom-call | flops 301989888 | bytes 1048576 | tf_op jit(solution)/shard_map/tiles/pallas_call | solution.py:236
  105.8 2.2 %collective-permute-start.38 = (f32[64,128]{1,0:T(8,128)S(1)}, f32[64,128]{1,0:T(8,128)S(1)}, u32[]{:S(2)}, u32[]{:S(2)}) collective-permute-start(f32[64,128]{1,0:T(8,128)S(1)} %add_add_fusion), channel_id=1, source_target_pairs={{0,3},{1,4},{2,5},{3,6},{4,7},{5,0},{6,1},{7,2},{8,11},{9,12},{10,... | collective-permute-start | bytes 98312 | tf_op jit(solution)/shard_map/ppermute | solution.py:48
  108.1 0.2 fusion.3
  108.3 4.9 %collective-permute-done.38 = f32[64,128]{1,0:T(8,128)S(1)} collective-permute-done((f32[64,128]{1,0:T(8,128)S(1)}, f32[64,128]{1,0:T(8,128)S(1)}, u32[]{:S(2)}, u32[]{:S(2)}) %collective-permute-start.38) | collective-permute-done | bytes 32800 | tf_op jit(solution)/shard_map/ppermute | solution.py:48
  113.2 0.2 fusion.1
  113.4 1.6 %fusion.2 = f32[32,1,64,128]{3,2,1,0:T(8,128)} fusion(f32[1,64,128]{2,1,0:T(8,128)S(1)} %bitcast.43, f32[15,64,128]{2,1,0:T(8,128)S(1)} %tiles.3, f32[16,64,128]{2,1,0:T(8,128)S(1)} %tiles.2, bf16[32,128,128]{2,1,0:T(8,128)(2,1)S(1)} %get-tuple-element.29, f32[64,128,1]{1,0,2:T(8,128)S(1)} %fusion.1), kind=kOutput, calls=%fused_computation.5 | convolution fusion | flops 403439616 | bytes 3178496 | tf_op jit(solution)/shard_map/rm,jmn->jrn/dot_general | solution.py:284
  (46 shorter events, 0.3 us)
Async XLA Ops:
  0.0 15.7 %collective-permute-start = (bf16[32,64,128]{2,1,0:T(8,128)(2,1)}, bf16[32,64,128]{2,1,0:T(8,128)(2,1)S(1)}, u32[]{:S(2)}, u32[]{:S(2)}) collective-permute-start(bf16[32,64,128]{2,1,0:T(8,128)(2,1)} %bitcast.37), channel_id=1, source_target_pairs={{192,0},{24,8},{208,16},{40,24},{224,32},{56,40},{240,48},{8,56},{... | collective-permute-start | bytes 1572872 | tf_op jit(solution)/shard_map/ppermute | solution.py:37
  1.5 22.8 %collective-permute-start.3 = (bf16[32,64,128]{2,1,0:T(8,128)(2,1)}, bf16[32,64,128]{2,1,0:T(8,128)(2,1)S(1)}, u32[]{:S(2)}, u32[]{:S(2)}) collective-permute-start(bf16[32,64,128]{2,1,0:T(8,128)(2,1)} %bitcast.38), channel_id=1, source_target_pairs={{64,0},{56,8},{80,16},{8,24},{96,32},{24,40},{112,48},{40,56},{128... | collective-permute-start | bytes 1572872 | tf_op jit(solution)/shard_map/ppermute | solution.py:37
  3.2 23.3 %collective-permute-start.17 = (bf16[32,64,128]{2,1,0:T(8,128)(2,1)}, bf16[32,64,128]{2,1,0:T(8,128)(2,1)S(1)}, u32[]{:S(2)}, u32[]{:S(2)}) collective-permute-start(bf16[32,64,128]{2,1,0:T(8,128)(2,1)} %bitcast.39), channel_id=1, source_target_pairs={{48,0},{72,8},{0,16},{88,24},{16,32},{104,40},{32,48},{120,56},{11... | collective-permute-start | bytes 1572872 | tf_op jit(solution)/shard_map/ppermute | solution.py:37
  5.6 8.3 %collective-permute-start.35 = (bf16[128,128]{1,0:T(8,128)(2,1)S(1)}, bf16[128,128]{1,0:T(8,128)(2,1)S(1)}, u32[]{:S(2)}, u32[]{:S(2)}) collective-permute-start(bf16[128,128]{1,0:T(8,128)(2,1)S(1)} %slice_bitcast_fusion), channel_id=1, source_target_pairs={{0,1},{1,2},{2,3},{3,4},{4,5},{5,6},{6,7},{7,0},{8,9},{9,10},{10,1... | collective-permute-start | bytes 98312 | tf_op jit(solution)/shard_map/ppermute | solution.py:48
  7.5 8.2 %collective-permute-start.37 = (bf16[128,128]{1,0:T(8,128)(2,1)S(1)}, bf16[128,128]{1,0:T(8,128)(2,1)S(1)}, u32[]{:S(2)}, u32[]{:S(2)}) collective-permute-start(bf16[128,128]{1,0:T(8,128)(2,1)S(1)} %slice_bitcast_fusion), channel_id=1, source_target_pairs={{0,2},{1,3},{2,4},{3,5},{4,6},{5,7},{6,0},{7,1},{8,10},{9,11},{10,... | collective-permute-start | bytes 98312 | tf_op jit(solution)/shard_map/ppermute | solution.py:48
  13.9 12.7 %collective-permute-start.18 = (bf16[32,64,128]{2,1,0:T(8,128)(2,1)}, bf16[32,64,128]{2,1,0:T(8,128)(2,1)S(1)}, u32[]{:S(2)}, u32[]{:S(2)}) collective-permute-start(bf16[32,64,128]{2,1,0:T(8,128)(2,1)} %bitcast.40), channel_id=1, source_target_pairs={{16,0},{200,8},{32,16},{216,24},{48,32},{232,40},{0,48},{248,56},{... | collective-permute-start | bytes 1572872 | tf_op jit(solution)/shard_map/ppermute | solution.py:37
  15.7 11.0 %collective-permute-start.22 = (bf16[32,64,128]{2,1,0:T(8,128)(2,1)}, bf16[32,64,128]{2,1,0:T(8,128)(2,1)S(1)}, u32[]{:S(2)}, u32[]{:S(2)}) collective-permute-start(bf16[32,64,128]{2,1,0:T(8,128)(2,1)} %bitcast.41), channel_id=1, source_target_pairs={{0,8},{8,0},{16,24},{24,16},{32,40},{40,32},{48,56},{56,48},{64,72... | collective-permute-start | bytes 1572872 | tf_op jit(solution)/shard_map/ppermute | solution.py:43
  15.7 7.6 %collective-permute-start.39 = (bf16[128,128]{1,0:T(8,128)(2,1)S(1)}, bf16[128,128]{1,0:T(8,128)(2,1)S(1)}, u32[]{:S(2)}, u32[]{:S(2)}) collective-permute-start(bf16[128,128]{1,0:T(8,128)(2,1)S(1)} %slice_bitcast_fusion), channel_id=1, source_target_pairs={{0,3},{1,4},{2,5},{3,6},{4,7},{5,0},{6,1},{7,2},{8,11},{9,12},{10,... | collective-permute-start | bytes 98312 | tf_op jit(solution)/shard_map/ppermute | solution.py:48
  23.3 10.4 %collective-permute-start.1 = (bf16[32,64,128]{2,1,0:T(8,128)(2,1)S(1)}, bf16[32,64,128]{2,1,0:T(8,128)(2,1)S(1)}, u32[]{:S(2)}, u32[]{:S(2)}) collective-permute-start(bf16[32,64,128]{2,1,0:T(8,128)(2,1)S(1)} %collective-permute-done.refs_1_), channel_id=1, source_target_pairs={{48,0},{72,8},{0,16},{88,24},{16,32},{104,40},{32,48},{120,56},{11... | collective-permute-start | bytes 1572872 | tf_op jit(solution)/shard_map/ppermute | solution.py:37
  24.3 14.3 %collective-permute-start.19 = (bf16[32,64,128]{2,1,0:T(8,128)(2,1)S(1)}, bf16[32,64,128]{2,1,0:T(8,128)(2,1)S(1)}, u32[]{:S(2)}, u32[]{:S(2)}) collective-permute-start(bf16[32,64,128]{2,1,0:T(8,128)(2,1)S(1)} %collective-permute-done.refs_1_), channel_id=1, source_target_pairs={{16,0},{200,8},{32,16},{216,24},{48,32},{232,40},{0,48},{248,56},{... | collective-permute-start | bytes 1572872 | tf_op jit(solution)/shard_map/ppermute | solution.py:37
  26.5 16.0 %collective-permute-start.6 = (bf16[32,64,128]{2,1,0:T(8,128)(2,1)S(1)}, bf16[32,64,128]{2,1,0:T(8,128)(2,1)S(1)}, u32[]{:S(2)}, u32[]{:S(2)}) collective-permute-start(bf16[32,64,128]{2,1,0:T(8,128)(2,1)S(1)} %collective-permute-done.refs_1_), channel_id=1, source_target_pairs={{192,0},{24,8},{208,16},{40,24},{224,32},{56,40},{240,48},{8,56},{... | collective-permute-start | bytes 1572872 | tf_op jit(solution)/shard_map/ppermute | solution.py:37
  26.6 15.9 %collective-permute-start.23 = (bf16[32,64,128]{2,1,0:T(8,128)(2,1)S(1)}, bf16[32,64,128]{2,1,0:T(8,128)(2,1)S(1)}, u32[]{:S(2)}, u32[]{:S(2)}) collective-permute-start(bf16[32,64,128]{2,1,0:T(8,128)(2,1)S(1)} %collective-permute-done.refs_1_), channel_id=1, source_target_pairs={{0,8},{8,0},{16,24},{24,16},{32,40},{40,32},{48,56},{56,48},{64,72... | collective-permute-start | bytes 1572872 | tf_op jit(solution)/shard_map/ppermute | solution.py:43
  26.7 17.5 %collective-permute-start.4 = (bf16[32,64,128]{2,1,0:T(8,128)(2,1)S(1)}, bf16[32,64,128]{2,1,0:T(8,128)(2,1)S(1)}, u32[]{:S(2)}, u32[]{:S(2)}) collective-permute-start(bf16[32,64,128]{2,1,0:T(8,128)(2,1)S(1)} %collective-permute-done.3.refs_2_), channel_id=1, source_target_pairs={{16,0},{200,8},{32,16},{216,24},{48,32},{232,40},{0,48},{248,56},{... | collective-permute-start | bytes 1572872 | tf_op jit(solution)/shard_map/ppermute | solution.py:37
  33.7 11.4 %collective-permute-start.20 = (bf16[32,64,128]{2,1,0:T(8,128)(2,1)S(1)}, bf16[32,64,128]{2,1,0:T(8,128)(2,1)S(1)}, u32[]{:S(2)}, u32[]{:S(2)}) collective-permute-start(bf16[32,64,128]{2,1,0:T(8,128)(2,1)S(1)} %collective-permute-done.3.refs_2_), channel_id=1, source_target_pairs={{48,0},{72,8},{0,16},{88,24},{16,32},{104,40},{32,48},{120,56},{11... | collective-permute-start | bytes 1572872 | tf_op jit(solution)/shard_map/ppermute | solution.py:37
  38.6 11.1 %collective-permute-start.21 = (bf16[32,64,128]{2,1,0:T(8,128)(2,1)S(1)}, bf16[32,64,128]{2,1,0:T(8,128)(2,1)S(1)}, u32[]{:S(2)}, u32[]{:S(2)}) collective-permute-start(bf16[32,64,128]{2,1,0:T(8,128)(2,1)S(1)} %collective-permute-done.17.refs_3_), channel_id=1, source_target_pairs={{48,0},{72,8},{0,16},{88,24},{16,32},{104,40},{32,48},{120,56},{11... | collective-permute-start | bytes 1572872 | tf_op jit(solution)/shard_map/ppermute | solution.py:37
  42.5 7.2 %collective-permute-start.24 = (bf16[32,64,128]{2,1,0:T(8,128)(2,1)S(1)}, bf16[32,64,128]{2,1,0:T(8,128)(2,1)S(1)}, u32[]{:S(2)}, u32[]{:S(2)}) collective-permute-start(bf16[32,64,128]{2,1,0:T(8,128)(2,1)S(1)} %collective-permute-done.3.refs_2_), channel_id=1, source_target_pairs={{0,8},{8,0},{16,24},{24,16},{32,40},{40,32},{48,56},{56,48},{64,72... | collective-permute-start | bytes 1572872 | tf_op jit(solution)/shard_map/ppermute | solution.py:43
  42.6 7.7 %collective-permute-start.25 = (bf16[32,64,128]{2,1,0:T(8,128)(2,1)S(1)}, bf16[32,64,128]{2,1,0:T(8,128)(2,1)S(1)}, u32[]{:S(2)}, u32[]{:S(2)}) collective-permute-start(bf16[32,64,128]{2,1,0:T(8,128)(2,1)S(1)} %collective-permute-done.17.refs_3_), channel_id=1, source_target_pairs={{0,8},{8,0},{16,24},{24,16},{32,40},{40,32},{48,56},{56,48},{64,72... | collective-permute-start | bytes 1572872 | tf_op jit(solution)/shard_map/ppermute | solution.py:43
  44.2 6.0 %collective-permute-start.26 = (bf16[32,64,128]{2,1,0:T(8,128)(2,1)S(1)}, bf16[32,64,128]{2,1,0:T(8,128)(2,1)S(1)}, u32[]{:S(2)}, u32[]{:S(2)}) collective-permute-start(bf16[32,64,128]{2,1,0:T(8,128)(2,1)S(1)} %collective-permute-done.18.refs_4_), channel_id=1, source_target_pairs={{0,8},{8,0},{16,24},{24,16},{32,40},{40,32},{48,56},{56,48},{64,72... | collective-permute-start | bytes 1572872 | tf_op jit(solution)/shard_map/ppermute | solution.py:43
  45.1 8.3 %collective-permute-start.27 = (bf16[32,64,128]{2,1,0:T(8,128)(2,1)S(1)}, bf16[32,64,128]{2,1,0:T(8,128)(2,1)S(1)}, u32[]{:S(2)}, u32[]{:S(2)}) collective-permute-start(bf16[32,64,128]{2,1,0:T(8,128)(2,1)S(1)} %collective-permute-done.1.refs_5_), channel_id=1, source_target_pairs={{0,8},{8,0},{16,24},{24,16},{32,40},{40,32},{48,56},{56,48},{64,72... | collective-permute-start | bytes 1572872 | tf_op jit(solution)/shard_map/ppermute | solution.py:43
  49.7 3.8 %collective-permute-start.28 = (bf16[32,64,128]{2,1,0:T(8,128)(2,1)S(1)}, bf16[32,64,128]{2,1,0:T(8,128)(2,1)S(1)}, u32[]{:S(2)}, u32[]{:S(2)}) collective-permute-start(bf16[32,64,128]{2,1,0:T(8,128)(2,1)S(1)} %collective-permute-done.19.refs_6_), channel_id=1, source_target_pairs={{0,8},{8,0},{16,24},{24,16},{32,40},{40,32},{48,56},{56,48},{64,72... | collective-permute-start | bytes 1572872 | tf_op jit(solution)/shard_map/ppermute | solution.py:43
  49.7 4.3 %collective-permute-start.31 = (bf16[32,64,128]{2,1,0:T(8,128)(2,1)S(1)}, bf16[32,64,128]{2,1,0:T(8,128)(2,1)S(1)}, u32[]{:S(2)}, u32[]{:S(2)}) collective-permute-start(bf16[32,64,128]{2,1,0:T(8,128)(2,1)S(1)} %collective-permute-done.6.refs_9_), channel_id=1, source_target_pairs={{0,8},{8,0},{16,24},{24,16},{32,40},{40,32},{48,56},{56,48},{64,72... | collective-permute-start | bytes 1572872 | tf_op jit(solution)/shard_map/ppermute | solution.py:43
  50.2 10.4 %collective-permute-start.7 = (bf16[32,64,128]{2,1,0:T(8,128)(2,1)S(1)}, bf16[32,64,128]{2,1,0:T(8,128)(2,1)S(1)}, u32[]{:S(2)}, u32[]{:S(2)}) collective-permute-start(bf16[32,64,128]{2,1,0:T(8,128)(2,1)S(1)} %collective-permute-done.6.refs_9_), channel_id=1, source_target_pairs={{48,0},{72,8},{0,16},{88,24},{16,32},{104,40},{32,48},{120,56},{11... | collective-permute-start | bytes 1572872 | tf_op jit(solution)/shard_map/ppermute | solution.py:37
  50.2 10.4 %collective-permute-start.9 = (bf16[32,64,128]{2,1,0:T(8,128)(2,1)S(1)}, bf16[32,64,128]{2,1,0:T(8,128)(2,1)S(1)}, u32[]{:S(2)}, u32[]{:S(2)}) collective-permute-start(bf16[32,64,128]{2,1,0:T(8,128)(2,1)S(1)} %collective-permute-done.6.refs_9_), channel_id=1, source_target_pairs={{16,0},{200,8},{32,16},{216,24},{48,32},{232,40},{0,48},{248,56},{... | collective-permute-start | bytes 1572872 | tf_op jit(solution)/shard_map/ppermute | solution.py:37
  53.5 10.4 %collective-permute-start.30 = (bf16[32,64,128]{2,1,0:T(8,128)(2,1)S(1)}, bf16[32,64,128]{2,1,0:T(8,128)(2,1)S(1)}, u32[]{:S(2)}, u32[]{:S(2)}) collective-permute-start(bf16[32,64,128]{2,1,0:T(8,128)(2,1)S(1)} %collective-permute-done.4.refs_8_), channel_id=1, source_target_pairs={{0,8},{8,0},{16,24},{24,16},{32,40},{40,32},{48,56},{56,48},{64,72... | collective-permute-start | bytes 1572872 | tf_op jit(solution)/shard_map/ppermute | solution.py:43
  53.5 10.5 %collective-permute-start.29 = (bf16[32,64,128]{2,1,0:T(8,128)(2,1)S(1)}, bf16[32,64,128]{2,1,0:T(8,128)(2,1)S(1)}, u32[]{:S(2)}, u32[]{:S(2)}) collective-permute-start(bf16[32,64,128]{2,1,0:T(8,128)(2,1)S(1)} %collective-permute-done.20.refs_7_), channel_id=1, source_target_pairs={{0,8},{8,0},{16,24},{24,16},{32,40},{40,32},{48,56},{56,48},{64,72... | collective-permute-start | bytes 1572872 | tf_op jit(solution)/shard_map/ppermute | solution.py:43
  54.0 19.8 %collective-permute-start.32 = (bf16[32,64,128]{2,1,0:T(8,128)(2,1)S(1)}, bf16[32,64,128]{2,1,0:T(8,128)(2,1)S(1)}, u32[]{:S(2)}, u32[]{:S(2)}) collective-permute-start(bf16[32,64,128]{2,1,0:T(8,128)(2,1)S(1)} %collective-permute-done.21.refs_10_), channel_id=1, source_target_pairs={{0,8},{8,0},{16,24},{24,16},{32,40},{40,32},{48,56},{56,48},{64,72... | collective-permute-start | bytes 1572872 | tf_op jit(solution)/shard_map/ppermute | solution.py:43
  60.6 13.7 %collective-permute-start.2 = (bf16[32,64,128]{2,1,0:T(8,128)(2,1)S(1)}, bf16[32,64,128]{2,1,0:T(8,128)(2,1)S(1)}, u32[]{:S(2)}, u32[]{:S(2)}) collective-permute-start(bf16[32,64,128]{2,1,0:T(8,128)(2,1)S(1)} %collective-permute-done.1.refs_5_), channel_id=1, source_target_pairs={{48,0},{72,8},{0,16},{88,24},{16,32},{104,40},{32,48},{120,56},{11... | collective-permute-start | bytes 1572872 | tf_op jit(solution)/shard_map/ppermute | solution.py:37
  60.6 13.8 %collective-permute-start.5 = (bf16[32,64,128]{2,1,0:T(8,128)(2,1)S(1)}, bf16[32,64,128]{2,1,0:T(8,128)(2,1)S(1)}, u32[]{:S(2)}, u32[]{:S(2)}) collective-permute-start(bf16[32,64,128]{2,1,0:T(8,128)(2,1)S(1)} %collective-permute-done.4.refs_8_), channel_id=1, source_target_pairs={{16,0},{200,8},{32,16},{216,24},{48,32},{232,40},{0,48},{248,56},{... | collective-permute-start | bytes 1572872 | tf_op jit(solution)/shard_map/ppermute | solution.py:37
  63.9 9.9 %collective-permute-start.8 = (bf16[16,64,128]{2,1,0:T(8,128)(2,1)S(1)}, bf16[16,64,128]{2,1,0:T(8,128)(2,1)S(1)}, u32[]{:S(2)}, u32[]{:S(2)}) collective-permute-start(bf16[16,64,128]{2,1,0:T(8,128)(2,1)S(1)} %split.8), channel_id=1, source_target_pairs={{48,0},{72,8},{0,16},{88,24},{16,32},{104,40},{32,48},{120,56},{11... | collective-permute-start | bytes 786440 | tf_op jit(solution)/shard_map/ppermute | solution.py:37
  64.0 10.8 %collective-permute-start.10 = (bf16[16,64,128]{2,1,0:T(8,128)(2,1)S(1)}, bf16[16,64,128]{2,1,0:T(8,128)(2,1)S(1)}, u32[]{:S(2)}, u32[]{:S(2)}) collective-permute-start(bf16[16,64,128]{2,1,0:T(8,128)(2,1)S(1)} %split.9), channel_id=1, source_target_pairs={{16,0},{200,8},{32,16},{216,24},{48,32},{232,40},{0,48},{248,56},{... | collective-permute-start | bytes 786440 | tf_op jit(solution)/shard_map/ppermute | solution.py:37
  73.8 1.5 %collective-permute-start.15 = (bf16[16,64,128]{2,1,0:T(8,128)(2,1)S(1)}, bf16[16,64,128]{2,1,0:T(8,128)(2,1)S(1)}, u32[]{:S(2)}, u32[]{:S(2)}) collective-permute-start(bf16[16,64,128]{2,1,0:T(8,128)(2,1)S(1)} %collective-permute-done.8.refs_2_), channel_id=1, source_target_pairs={{0,8},{8,0},{16,24},{24,16},{32,40},{40,32},{48,56},{56,48},{64,72... | collective-permute-start | bytes 786440 | tf_op jit(solution)/shard_map/ppermute | solution.py:43
  73.8 13.0 %collective-permute-start.11 = (bf16[32,64,128]{2,1,0:T(8,128)(2,1)S(1)}, bf16[32,64,128]{2,1,0:T(8,128)(2,1)S(1)}, u32[]{:S(2)}, u32[]{:S(2)}) collective-permute-start(bf16[32,64,128]{2,1,0:T(8,128)(2,1)S(1)} %collective-permute-done.7.refs_11_), channel_id=1, source_target_pairs={{0,8},{8,0},{16,24},{24,16},{32,40},{40,32},{48,56},{56,48},{64,72... | collective-permute-start | bytes 1572872 | tf_op jit(solution)/shard_map/ppermute | solution.py:43
  74.3 12.5 %collective-permute-start.12 = (bf16[32,64,128]{2,1,0:T(8,128)(2,1)S(1)}, bf16[32,64,128]{2,1,0:T(8,128)(2,1)S(1)}, u32[]{:S(2)}, u32[]{:S(2)}) collective-permute-start(bf16[32,64,128]{2,1,0:T(8,128)(2,1)S(1)} %collective-permute-done.9.refs_12_), channel_id=1, source_target_pairs={{0,8},{8,0},{16,24},{24,16},{32,40},{40,32},{48,56},{56,48},{64,72... | collective-permute-start | bytes 1572872 | tf_op jit(solution)/shard_map/ppermute | solution.py:43
  74.4 12.4 %collective-permute-start.13 = (bf16[32,64,128]{2,1,0:T(8,128)(2,1)S(1)}, bf16[32,64,128]{2,1,0:T(8,128)(2,1)S(1)}, u32[]{:S(2)}, u32[]{:S(2)}) collective-permute-start(bf16[32,64,128]{2,1,0:T(8,128)(2,1)S(1)} %collective-permute-done.2.refs_0_), channel_id=1, source_target_pairs={{0,8},{8,0},{16,24},{24,16},{32,40},{40,32},{48,56},{56,48},{64,72... | collective-permute-start | bytes 1572872 | tf_op jit(solution)/shard_map/ppermute | solution.py:43
  74.8 12.0 %collective-permute-start.14 = (bf16[32,64,128]{2,1,0:T(8,128)(2,1)S(1)}, bf16[32,64,128]{2,1,0:T(8,128)(2,1)S(1)}, u32[]{:S(2)}, u32[]{:S(2)}) collective-permute-start(bf16[32,64,128]{2,1,0:T(8,128)(2,1)S(1)} %collective-permute-done.5.refs_1_), channel_id=1, source_target_pairs={{0,8},{8,0},{16,24},{24,16},{32,40},{40,32},{48,56},{56,48},{64,72... | collective-permute-start | bytes 1572872 | tf_op jit(solution)/shard_map/ppermute | solution.py:43
  75.3 3.4 %collective-permute-start.16 = (bf16[16,64,128]{2,1,0:T(8,128)(2,1)S(1)}, bf16[16,64,128]{2,1,0:T(8,128)(2,1)S(1)}, u32[]{:S(2)}, u32[]{:S(2)}) collective-permute-start(bf16[16,64,128]{2,1,0:T(8,128)(2,1)S(1)} %collective-permute-done.10.refs_3_), channel_id=1, source_target_pairs={{0,8},{8,0},{16,24},{24,16},{32,40},{40,32},{48,56},{56,48},{64,72... | collective-permute-start | bytes 786440 | tf_op jit(solution)/shard_map/ppermute | solution.py:43
  78.7 9.5 %collective-permute-start.41 = (f32[128,128]{0,1:T(8,128)S(1)}, f32[128,128]{0,1:T(8,128)S(1)}, u32[]{:S(2)}, u32[]{:S(2)}) collective-permute-start(f32[128,128]{0,1:T(8,128)S(1)} %bitcast.47), channel_id=1, source_target_pairs={{0,3},{1,4},{2,5},{3,6},{4,7},{5,0},{6,1},{7,2},{8,11},{9,12},{10,... | collective-permute-start | bytes 196616 | tf_op jit(solution)/shard_map/ppermute | solution.py:48
  81.1 1.0 copy-start
  88.2 7.3 %collective-permute-start.36 = (f32[64,128]{1,0:T(8,128)S(1)}, f32[64,128]{1,0:T(8,128)S(1)}, u32[]{:S(2)}, u32[]{:S(2)}) collective-permute-start(f32[64,128]{1,0:T(8,128)S(1)} %get-tuple-element.28), channel_id=1, source_target_pairs={{0,3},{1,4},{2,5},{3,6},{4,7},{5,0},{6,1},{7,2},{8,11},{9,12},{10,... | collective-permute-start | bytes 98312 | tf_op jit(solution)/shard_map/ppermute | solution.py:48
  88.6 8.2 %collective-permute-start.34 = (f32[64,128]{1,0:T(8,128)S(1)}, f32[64,128]{1,0:T(8,128)S(1)}, u32[]{:S(2)}, u32[]{:S(2)}) collective-permute-start(f32[64,128]{1,0:T(8,128)S(1)} %get-tuple-element.28), channel_id=1, source_target_pairs={{0,2},{1,3},{2,4},{3,5},{4,6},{5,7},{6,0},{7,1},{8,10},{9,11},{10,... | collective-permute-start | bytes 98312 | tf_op jit(solution)/shard_map/ppermute | solution.py:48
  92.6 4.4 %collective-permute-start.33 = (f32[64,128]{1,0:T(8,128)S(1)}, f32[64,128]{1,0:T(8,128)S(1)}, u32[]{:S(2)}, u32[]{:S(2)}) collective-permute-start(f32[64,128]{1,0:T(8,128)S(1)} %get-tuple-element.28), channel_id=1, source_target_pairs={{0,1},{1,2},{2,3},{3,4},{4,5},{5,6},{6,7},{7,0},{8,9},{9,10},{10,1... | collective-permute-start | bytes 98312 | tf_op jit(solution)/shard_map/ppermute | solution.py:48
  97.0 11.0 %collective-permute-start.40 = (f32[64,128]{1,0:T(8,128)S(1)}, f32[64,128]{1,0:T(8,128)S(1)}, u32[]{:S(2)}, u32[]{:S(2)}) collective-permute-start(f32[64,128]{1,0:T(8,128)S(1)} %add_add_fusion), channel_id=1, source_target_pairs={{0,6},{1,7},{2,0},{3,1},{4,2},{5,3},{6,4},{7,5},{8,14},{9,15},{10,... | collective-permute-start | bytes 98312 | tf_op jit(solution)/shard_map/ppermute | solution.py:48
  105.8 7.4 %collective-permute-start.38 = (f32[64,128]{1,0:T(8,128)S(1)}, f32[64,128]{1,0:T(8,128)S(1)}, u32[]{:S(2)}, u32[]{:S(2)}) collective-permute-start(f32[64,128]{1,0:T(8,128)S(1)} %add_add_fusion), channel_id=1, source_target_pairs={{0,3},{1,4},{2,5},{3,6},{4,7},{5,0},{6,1},{7,2},{8,11},{9,12},{10,... | collective-permute-start | bytes 98312 | tf_op jit(solution)/shard_map/ppermute | solution.py:48
